TPU v7x, 32 devices: a whole 2x2x4 slice. The times are simulated.
32 devices in a mesh: grp: 2 (over x), seq: 8 (over z, y), col: 2 (over core).
Axes of the slice: x: 2, y: 2, z: 4, core: 2. Of those that a mesh axis runs over, the one named last changes fastest.
Arguments:
- signal: bfloat16 [8192, 1408], P(('grp', 'seq'), 'col'), parts along dimension 0, may hold values from -6 to 6
- conv_weight: bfloat16 [5, 1408, 1408], P(None, None, 'col'), may hold values from -0.15625 to 0.15625
- conv_gain: float32 [1408], replicated, may hold values from 0.1 to 1.9
- embed_weight: bfloat16 [1408, 1536], P('col', 'seq'), may hold values from -0.15625 to 0.15625
- attn_gain: float32 [1536], replicated, may hold values from 0.1 to 1.9
- query_weight: bfloat16 [1536, 1024], P('seq'), may hold values from -4 to 4
- keyvalue_weight: bfloat16 [1536, 320], P('seq'), may hold values from -4 to 4
- output_weight: bfloat16 [1536, 1536], P(None, 'seq'), may hold values from -0.15625 to 0.15625
- rowcol_weight: bfloat16 [1536, 256], replicated, may hold values from -0.15625 to 0.15625
- pair_weight: bfloat16 [128, 128], replicated, may hold values from -0.5 to 0.5
Outputs:
- tokens: bfloat16 [2048, 1536], P(('grp', 'seq', 'col')), parts along dimension 0
- pair_out: bfloat16 [128, 64, 128], P(('grp', 'seq'), 'col'), parts along dimension 0
There are 2 independent parts, one for each index of `grp`. A program takes and returns all parts, laid end to end along the dimension named above; an argument that names none is the same for every part. Nothing has to cross between parts.
All inputs are finite; a program needn't handle non-finite values.
Results may differ from a plain program's by a relative error of at most 0.015.
Values may be sent and summed in bfloat16 or wider, within the bound.
A program may use at most 128 MiB of HBM per device.

v0:
```python
import jax
import jax.numpy as jnp
from jax import lax
from jax.sharding import PartitionSpec as P

DK = 128
DV = 192
POOL = 4
PAIR_POOL = 16


def with_halo(array, sides, width):
    for axis, dim in sides:
        size, length = (lax.axis_size(axis), array.shape[dim])
        up = [(i, (i + 1) % size) for i in range(size - 1)]
        down = [(j, i) for i, j in up]
        last = lax.slice_in_dim(array, length - width, length, axis=dim)
        first = lax.slice_in_dim(array, 0, width, axis=dim)
        before = lax.ppermute(last, axis, up)
        after = lax.ppermute(first, axis, down)
        array = jnp.concatenate([before, array, after], axis=dim)
    return array


def rms_scale(values, gain_vector):
    return (
        values * lax.rsqrt(jnp.mean(values * values, axis=-1, keepdims=True) + 1e-06) * gain_vector
    )


def attention_parts(queries, head_count):
    query_rows = queries.reshape(queries.shape[0] * head_count, DK)

    def absorb(running, pieces, first_row):
        running_max, running_sum, accumulated = running
        key_piece, value_piece = pieces
        scores = lax.dot_general(
            query_rows, key_piece, (((1,), (1,)), ((), ())), preferred_element_type=jnp.float32
        )
        newest_max = jnp.maximum(running_max, jnp.max(scores, axis=1))
        weights = jnp.exp(scores - newest_max[:, None])
        running_sum = jnp.sum(weights, axis=1)
        accumulated = jnp.dot(
            weights.astype(jnp.bfloat16), value_piece, preferred_element_type=jnp.float32
        )
        return (newest_max, running_sum, accumulated)

    row_count = query_rows.shape[0]
    initial = (
        jnp.full((row_count,), -1e30, jnp.float32),
        jnp.zeros((row_count,), jnp.float32),
        jnp.zeros((row_count, DV), jnp.float32),
    )
    return (absorb, initial)


def finish_attention(result, token_count):
    running_max, running_sum, accumulated = result
    return (accumulated / running_sum[:, None]).astype(jnp.bfloat16).reshape(token_count, -1)


def on_device(
    signal,
    conv_weight,
    conv_gain,
    embed_weight,
    attn_gain,
    query_weight,
    keyvalue_weight,
    output_weight,
    rowcol_weight,
    pair_weight,
):
    positions = signal.shape[0]
    tap_count = conv_weight.shape[0]
    halo_width = tap_count // 2
    padded = with_halo(signal, (("seq", 0),), halo_width)
    widened = lax.all_gather(padded, "col", axis=1, tiled=True)
    activated = jax.nn.gelu(
        rms_scale(widened.astype(jnp.float32), conv_gain), approximate=True
    ).astype(jnp.bfloat16)
    summed = signal.astype(jnp.float32)
    for tap_index in range(tap_count):
        summed = summed + jnp.dot(
            activated[tap_index : tap_index + positions],
            conv_weight[tap_index],
            preferred_element_type=jnp.float32,
        )
    pooled = jnp.mean(summed.reshape(positions // POOL, POOL, -1), axis=1).astype(jnp.bfloat16)
    embed_full = lax.all_gather(embed_weight, "seq", axis=1, tiled=True)
    col_count = lax.axis_size("col")
    embedded = lax.psum_scatter(
        jnp.dot(pooled, embed_full, preferred_element_type=jnp.float32).astype(jnp.bfloat16),
        "col",
        scatter_dimension=0,
        tiled=True,
    )
    normed = rms_scale(embedded.astype(jnp.float32), attn_gain).astype(jnp.bfloat16)
    head_count = query_weight.shape[1] // DK
    scaling = DK ** (-0.5)
    col_index = lax.axis_index("col")
    local_heads = head_count // col_count
    group_tokens = lax.all_gather(normed, "col", axis=0, tiled=True)
    group_count = group_tokens.shape[0]
    query_half = lax.dynamic_slice_in_dim(
        query_weight, col_index * local_heads * DK, local_heads * DK, 1
    )
    query_sum = jnp.dot(
        group_tokens,
        lax.all_gather(query_half, "seq", axis=0, tiled=True),
        preferred_element_type=jnp.float32,
    )
    keyvalue_sum = jnp.dot(
        group_tokens,
        lax.all_gather(keyvalue_weight, "seq", axis=0, tiled=True),
        preferred_element_type=jnp.float32,
    )
    queries = (query_sum * scaling).astype(jnp.bfloat16)
    keyvalue = keyvalue_sum.astype(jnp.bfloat16)
    absorb, initial = attention_parts(queries, local_heads)
    result = absorb(
        initial,
        (
            lax.all_gather(keyvalue[:, :DK], "seq", axis=0, tiled=True),
            lax.all_gather(keyvalue[:, DK:], "seq", axis=0, tiled=True),
        ),
        jnp.int32(0),
    )
    attended = finish_attention(result, group_count)
    output_half = lax.dynamic_slice_in_dim(
        output_weight, col_index * local_heads * DV, local_heads * DV, 0
    )
    partial_out = jnp.dot(
        attended,
        lax.all_gather(output_half, "seq", axis=1, tiled=True),
        preferred_element_type=jnp.float32,
    )
    attention_out = lax.psum_scatter(
        partial_out.astype(jnp.bfloat16), "col", scatter_dimension=0, tiled=True
    ).astype(jnp.float32)
    tokens = (embedded.astype(jnp.float32) + attention_out).astype(jnp.bfloat16)
    pair_pool = jnp.mean(
        tokens.astype(jnp.float32).reshape(-1, PAIR_POOL, tokens.shape[1]), axis=1
    ).astype(jnp.bfloat16)
    projected = jnp.dot(pair_pool, rowcol_weight, preferred_element_type=jnp.float32).astype(
        jnp.bfloat16
    )
    features = pair_weight.shape[0]
    row_block = lax.all_gather(projected, "col", axis=0, tiled=True)
    column_all = lax.all_gather(row_block[:, features:], "seq", axis=0, tiled=True)
    row_part = row_block[:, :features]
    column_span = column_all.shape[0] // col_count
    column_part = lax.dynamic_slice_in_dim(
        column_all, lax.axis_index("col") * column_span, column_span, 0
    )
    hidden = jax.nn.gelu(
        row_part.astype(jnp.float32)[:, None, :] + column_part.astype(jnp.float32)[None, :, :],
        approximate=True,
    ).astype(jnp.bfloat16)
    pair_out = jnp.dot(
        hidden.reshape(-1, features), pair_weight, preferred_element_type=jnp.float32
    ).astype(jnp.bfloat16)
    return (tokens, pair_out.reshape(row_part.shape[0], column_span, features))


def solution(mesh):
    placed = (
        P(("grp", "seq"), "col"),
        P(None, None, "col"),
        P(),
        P("col", "seq"),
        P(),
        P("seq", None),
        P("seq", None),
        P(None, "seq"),
        P(),
        P(),
    )
    return jax.shard_map(
        on_device,
        mesh=mesh,
        in_specs=placed,
        out_specs=(P(("grp", "seq", "col"), None), P(("grp", "seq"), "col", None)),
        check_vma=False,
    )
```

profile of v0, /device:TPU:0, one launch (start us, length us, event | category | flops | bytes accessed | tf_op | source)
XLA Modules:
  0.0 256.0 jit_solution(12248278608278916954)
XLA Ops:
  7.2 1.4 copy.19
  8.7 4.9 %collective-permute-start = (bf16[2,704]{1,0:T(2,128)(2,1)S(1)}, bf16[2,704]{1,0:T(2,128)(2,1)S(1)}, u32[]{:S(2)}, u32[]{:S(2)}) collective-permute-start(bf16[2,704]{1,0:T(2,128)(2,1)S(1)} %get-tuple-element.4), channel_id=1, source_target_pairs={{0,2},{2,4},{4,6},{6,8},{8,10},{10,12},{12,14},{1,3},{3,5},{5,7},{... | collective-permute-start | bytes 8456 | tf_op jit(solution)/shard_map/ppermute | solution.py:19
  14.9 4.2 %collective-permute-done.1 = bf16[2,704]{1,0:T(2,128)(2,1)S(1)} collective-permute-done((bf16[2,704]{1,0:T(2,128)(2,1)S(1)}, bf16[2,704]{1,0:T(2,128)(2,1)S(1)}, u32[]{:S(2)}, u32[]{:S(2)}) %collective-permute-start.1) | collective-permute-done | bytes 2848 | tf_op jit(solution)/shard_map/ppermute | solution.py:20
  21.0 10.3 %all-gather.13.cloned.1.call-done = bf16[2,704,516]{1,2,0:T(8,128)(2,1)} async-done(((bf16[1,704,516]{1,2,0:T(8,128)(2,1)}), bf16[2,704,516]{1,2,0:T(8,128)(2,1)}) %all-gather.13.cloned.1.call-update) | async-done | bytes 1453072 | tf_op jit(solution)/shard_map/all_gather | solution.py:78
  31.4 4.3 %copy.22 = f32[2,704,516]{1,0,2:T(2,128)} copy(bf16[2,704,516]{1,2,0:T(8,128)(2,1)} %all-gather.13.cloned.1.call-done) | data formatting | bytes 4359168 | tf_op jit(solution)/shard_map/convert_element_type | solution.py:80
  35.6 5.3 %reshape.62 = f32[1408,516]{0,1:T(8,128)} reshape(f32[2,704,516]{1,0,2:T(2,128)} %copy.22) | data formatting | bytes 5812224 | tf_op jit(solution)/shard_map/convert_element_type | solution.py:80
  41.0 2.4 multiply_reduce_fusion
  45.1 3.0 %fusion.16 = f32[512,704]{0,1:T(8,128)S(1)} fusion(bf16[5,1408,704]{1,2,0:T(8,128)(2,1)} %param.11, bf16[516,1408]{1,0:T(8,128)(2,1)S(1)} %fusion.7), kind=kOutput, calls=%fused_computation.21 | convolution fusion | flops 1015021568 | bytes 4866048 | tf_op jit(solution)/shard_map/dot_general | solution.py:84
  53.6 1.5 add_add_fusion
  55.1 1.6 copy.23
  56.7 1.8 reshape.50
  59.5 27.1 %all-gather.7.cloned.1.call-done = bf16[704,1536]{0,1:T(8,128)(2,1)} async-done(((bf16[704,192]{0,1:T(8,128)(2,1)}), bf16[704,1536]{0,1:T(8,128)(2,1)}) %all-gather.7.cloned.1.call-update) | async-done | bytes 2162704 | tf_op jit(solution)/shard_map/all_gather | solution.py:90
  86.6 3.3 %convolution_convert_fusion.1 = bf16[128,1536]{1,0:T(8,128)(2,1)} fusion(bf16[704,1536]{0,1:T(8,128)(2,1)} %all-gather.7.cloned.1.call-done, f32[128,704]{1,0:T(8,128)S(1)} %reduce_sum.46), kind=kOutput, calls=%fused_computation.11 | convolution fusion | flops 277200896 | bytes 2916352 | tf_op jit(solution)/shard_map/dot_general | solution.py:93
  91.6 34.7 %all_gather.34 = bf16[1536,320]{1,0:T(8,128)(2,1)S(1)} all-gather(bf16[192,320]{1,0:T(8,128)(2,1)S(1)} %copy-done.6), channel_id=1, replica_groups=mesh['grp'=2,'seq'=8,'col'=2] {'seq'}, dimensions={0}, use_global_device_ids=true | all-gather | bytes 1105920 | tf_op jit(solution)/shard_map/all_gather | solution.py:115
  128.4 2.3 all_gather.32
  131.2 17.2 %all-gather.9.cloned.1.call-done = bf16[1536,512]{1,0:T(8,128)(2,1)} async-done(((bf16[192,512]{1,0:T(8,128)(2,1)}), bf16[1536,512]{1,0:T(8,128)(2,1)}) %all-gather.9.cloned.1.call-update) | async-done | bytes 1572880 | tf_op jit(solution)/shard_map/all_gather | solution.py:110
  148.5 1.8 fusion.35
  150.4 27.6 %all_gather.35 = bf16[1024,128]{0,1:T(8,128)(2,1)S(1)} all-gather(bf16[128,128]{0,1:T(8,128)(2,1)S(1)} %slice.71), channel_id=1, replica_groups=mesh['grp'=2,'seq'=8,'col'=2] {'seq'}, dimensions={0}, use_global_device_ids=true | all-gather | bytes 294912 | tf_op jit(solution)/shard_map/all_gather | solution.py:124
  177.9 29.5 %all_gather.36 = bf16[1024,192]{0,1:T(8,128)(2,1)S(1)} all-gather(bf16[128,192]{0,1:T(8,128)(2,1)S(1)} %slice.72), channel_id=1, replica_groups=mesh['grp'=2,'seq'=8,'col'=2] {'seq'}, dimensions={0}, use_global_device_ids=true | all-gather | bytes 442368 | tf_op jit(solution)/shard_map/all_gather | solution.py:125
  209.6 3.3 %convolution_convert_fusion = bf16[128,1536]{1,0:T(8,128)(2,1)} fusion(bf16[128,768]{1,0:T(8,128)(2,1)S(1)} %reshape.52, bf16[768,1536]{0,1:T(8,128)(2,1)} %all-gather.11.cloned.1.call-done), kind=kOutput, calls=%fused_computation.10 | convolution fusion | flops 302186496 | bytes 2949120 | tf_op jit(solution)/shard_map/dot_general | solution.py:133
  212.9 5.2 %reduce-scatter.5.cloned.1.call-done = bf16[64,1536]{1,0:T(8,128)(2,1)} async-done(((bf16[128,1536]{1,0:T(8,128)(2,1)}), bf16[64,1536]{1,0:T(8,128)(2,1)}) %reduce-scatter.5.cloned.1.call-update) | async-done | bytes 196624 | tf_op jit(solution)/shard_map/reduce_scatter | solution.py:138
  218.1 1.7 convert_reduce_fusion
  220.0 1.8 all-gather.1
  221.9 26.4 %all_gather.39 = bf16[64,128]{1,0:T(8,128)(2,1)S(1)} all-gather(bf16[8,128]{1,0:T(8,128)(2,1)S(1)} %get-tuple-element.7), channel_id=1, replica_groups=mesh['grp'=2,'seq'=8,'col'=2] {'seq'}, dimensions={0}, use_global_device_ids=true | all-gather | bytes 18432 | tf_op jit(solution)/shard_map/all_gather | solution.py:150
  (68 shorter events, 19.0 us)
Async XLA Ops:
  7.2 212.6 %copy-start = (bf16[1536,256]{1,0:T(8,128)(2,1)S(1)}, bf16[1536,256]{1,0:T(8,128)(2,1)}, u32[]{:S(2)}) copy-start(bf16[1536,256]{1,0:T(8,128)(2,1)} %param.18) | copy-start | bytes 2359300
  7.2 24.2 %all-gather.13.cloned.1.call-start = ((), (), s32[]{:S(2)}) async-start(), calls=%async_computation.7 | async-start | bytes 2396160 | tf_op jit(solution)/shard_map/all_gather | solution.py:78
  8.7 6.2 %collective-permute-start = (bf16[2,704]{1,0:T(2,128)(2,1)S(1)}, bf16[2,704]{1,0:T(2,128)(2,1)S(1)}, u32[]{:S(2)}, u32[]{:S(2)}) collective-permute-start(bf16[2,704]{1,0:T(2,128)(2,1)S(1)} %get-tuple-element.4), channel_id=1, source_target_pairs={{0,2},{2,4},{4,6},{6,8},{8,10},{10,12},{12,14},{1,3},{3,5},{5,7},{... | collective-permute-start | bytes 8456 | tf_op jit(solution)/shard_map/ppermute | solution.py:19
  13.6 5.5 %collective-permute-start.1 = (bf16[2,704]{1,0:T(2,128)(2,1)S(1)}, bf16[2,704]{1,0:T(2,128)(2,1)S(1)}, u32[]{:S(2)}, u32[]{:S(2)}) collective-permute-start(bf16[2,704]{1,0:T(2,128)(2,1)S(1)} %get-tuple-element.5), channel_id=1, source_target_pairs={{2,0},{4,2},{6,4},{8,6},{10,8},{12,10},{14,12},{3,1},{5,3},{7,5},{... | collective-permute-start | bytes 8456 | tf_op jit(solution)/shard_map/ppermute | solution.py:20
  20.2 66.3 %all-gather.7.cloned.1.call-start = ((), (), s32[]{:S(2)}) async-start(), calls=%async_computation.2 | async-start | bytes 2654208 | tf_op jit(solution)/shard_map/all_gather | solution.py:90
  21.0 105.3 %reduce-scatter.3.cloned.1.call-start = ((), (), s32[]{:S(2)}) async-start(), calls=%async_computation.3 | async-start | bytes 589824 | tf_op jit(solution)/shard_map/reduce_scatter | solution.py:92
  41.0 2.9 %copy-start.1 = (f32[1408,516]{0,1:T(8,128)S(1)}, f32[1408,516]{0,1:T(8,128)}, u32[]{:S(2)}) copy-start(f32[1408,516]{0,1:T(8,128)} %reshape.62) | copy-start | bytes 8718340
  41.0 2.9 %copy-start.9 = (f32[1408]{0:T(1024)S(1)}, f32[1408]{0:T(1024)}, u32[]{:S(2)}) copy-start(f32[1408]{0:T(1024)} %param.12) | copy-start | bytes 16900
  45.1 4.4 %copy-start.4 = (bf16[5,1408,704]{1,2,0:T(8,128)(2,1)S(1)}, bf16[5,1408,704]{1,2,0:T(8,128)(2,1)}, u32[]{:S(2)}) copy-start(bf16[5,1408,704]{1,2,0:T(8,128)(2,1)} %param.11) | copy-start | bytes 29736964
  52.2 1.4 copy-start.2
  59.4 30.5 %copy-start.7 = (bf16[192,1024]{1,0:T(8,128)(2,1)S(1)}, bf16[192,1024]{1,0:T(8,128)(2,1)}, u32[]{:S(2)}) copy-start(bf16[192,1024]{1,0:T(8,128)(2,1)} %param.15) | copy-start | bytes 1179652
  59.4 31.3 %copy-start.5 = (bf16[1536,192]{0,1:T(8,128)(2,1)S(1)}, bf16[1536,192]{0,1:T(8,128)(2,1)}, u32[]{:S(2)}) copy-start(bf16[1536,192]{0,1:T(8,128)(2,1)} %param.17) | copy-start | bytes 1769476
  59.4 32.1 %copy-start.6 = (bf16[192,320]{1,0:T(8,128)(2,1)S(1)}, bf16[192,320]{1,0:T(8,128)(2,1)}, u32[]{:S(2)}) copy-start(bf16[192,320]{1,0:T(8,128)(2,1)} %param.16) | copy-start | bytes 368644
  89.9 37.5 %copy-start.10 = (f32[1536]{0:T(1024)S(1)}, f32[1536]{0:T(1024)}, u32[]{:S(2)}) copy-start(f32[1536]{0:T(1024)} %param.14) | copy-start | bytes 18436
  89.9 58.6 %all-gather.9.cloned.1.call-start = ((), (), s32[]{:S(2)}) async-start(), calls=%async_computation.4 | async-start | bytes 1769472 | tf_op jit(solution)/shard_map/all_gather | solution.py:110
  90.7 118.9 %all-gather.11.cloned.1.call-start = ((), (), s32[]{:S(2)}) async-start(), calls=%async_computation.5 | async-start | bytes 2654208 | tf_op jit(solution)/shard_map/all_gather | solution.py:135
  91.5 126.6 %reduce-scatter.5.cloned.1.call-start = ((), (), s32[]{:S(2)}) async-start(), calls=%async_computation.6 | async-start | bytes 589824 | tf_op jit(solution)/shard_map/reduce_scatter | solution.py:138
  209.2 8.9 %copy-start.3 = (bf16[64,1536]{1,0:T(8,128)(2,1)S(1)}, bf16[64,1536]{1,0:T(8,128)(2,1)}, u32[]{:S(2)}) copy-start(bf16[64,1536]{1,0:T(8,128)(2,1)} %reduce-scatter.3.cloned.1.call-done) | copy-start | bytes 589828
  209.5 38.8 %copy-start.8 = (bf16[128,128]{1,0:T(8,128)(2,1)S(1)}, bf16[128,128]{1,0:T(8,128)(2,1)}, u32[]{:S(2)}) copy-start(bf16[128,128]{1,0:T(8,128)(2,1)} %param.19) | copy-start | bytes 98308
Sparse Core Ops, SparseCore 0:
  20.3 10.9 all-gather.12
  33.5 52.9 all-gather.6
  90.0 6.3 reduce-scatter.2
  99.0 49.4 all-gather.8
  150.5 55.1 all-gather.10
  213.0 5.0 reduce-scatter.4
where the time goes:
time: 257 us; the launch traced here: 256 us
  blocking collectives  122 us (47%)
  waiting for transfers between devices  64.9 us (25%)
  matrix products  19.5 us (8%)
  local copies, waits for them, and re-layouts  18.4 us (7%)
  between operations  14.4 us (6%)
  other arithmetic  10.1 us (4%)
  starting transfers between devices  6.43 us (3%)
    all_gather x1, blocking collectives, on_device(): lax.all_gather(keyvalue_weight, 'seq', axis=0, tiled=True)  34.7 us
    all_gather x1, blocking collectives, on_device(): lax.all_gather(keyvalue[:, DK:], 'seq', axis=0, tiled=True)  29.5 us
    all_gather x1, blocking collectives, on_device(): lax.all_gather(keyvalue[:, :DK], 'seq', axis=0, tiled=True)  27.6 us
    all_gather x1, waiting for transfers between devices, on_device(): embed_full = lax.all_gather(embed_weight, 'seq', axis=1, tiled=True)  27.1 us
    all_gather x1, blocking collectives, on_device(): lax.all_gather(row_block[:, features:], 'seq', axis=0, tiled=True)  26.4 us
    all_gather x1, waiting for transfers between devices, on_device(): lax.all_gather(query_half, 'seq', axis=0, tiled=True)  17.2 us
    all_gather x1, waiting for transfers between devices, on_device(): widened = lax.all_gather(padded, 'col', axis=1, tiled=True)  10.3 us
    convert_element_type x2, local copies, waits for them, and re-layouts, on_device(): widened.astype(jnp.float32)  9.6 us
  transfers between devices with their start and end apart: 8, of which 5 were waited for; matrix products, arithmetic and copies ran while one was open for 13% of the time, Pallas kernels for 0%

commit v1 on v0

--- a/solution.py
+++ b/solution.py
@@ -7,6 +7,11 @@
 DV = 192
 POOL = 4
 PAIR_POOL = 16
+
+
+def exchange_gather(x, name, along):
+    sent = jnp.stack([x] * lax.axis_size(name))
+    return jnp.concatenate(lax.all_to_all(sent, name, 0, 0), axis=along)
 
 
 def with_halo(array, sides, width):
@@ -106,9 +111,7 @@
         query_weight, col_index * local_heads * DK, local_heads * DK, 1
     )
     query_sum = jnp.dot(
-        group_tokens,
-        lax.all_gather(query_half, "seq", axis=0, tiled=True),
-        preferred_element_type=jnp.float32,
+        group_tokens, exchange_gather(query_half, "seq", 0), preferred_element_type=jnp.float32
     )
     keyvalue_sum = jnp.dot(
         group_tokens,

time: 257 us -> 278 us (1.082)
  blocking collectives: 122 us -> 158 us
  waiting for transfers between devices: 64.9 us -> 47.7 us
  starting transfers between devices: 6.43 us -> 10.1 us
    all_gather x1, blocking collectives: 34.7 us -> 73.4 us  [on_device(): lax.all_gather(keyvalue_weight, 'seq', axis=0, tiled=True)]
    all_gather x1 -> x0, waiting for transfers between devices: 17.2 us -> none  [on_device(): lax.all_gather(query_half, 'seq', axis=0, tiled=True)]
    all_to_all x0 -> x1, starting transfers between devices: none -> 3.71 us  [exchange_gather(): return jnp.concatenate(lax.all_to_all(sent, name, 0, 0), axis=along)]
  transfers between devices with their start and end apart: 8 -> 8, of which waited for: 5 -> 4; matrix products, arithmetic and copies ran while one was open for 13% -> 12% of each run, Pallas kernels for 0% -> 0%
where the time goes in v1:
time: 278 us
  blocking collectives  158 us (57%)
  waiting for transfers between devices  47.7 us (17%)
  local copies, waits for them, and re-layouts  19.2 us (7%)
  matrix products  19.1 us (7%)
  between operations  14.1 us (5%)
  starting transfers between devices  10.1 us (4%)
  other arithmetic  10.1 us (4%)
    all_gather x1, blocking collectives, on_device(): lax.all_gather(keyvalue_weight, 'seq', axis=0, tiled=True)  73.4 us
    all_gather x1, blocking collectives, on_device(): lax.all_gather(keyvalue[:, DK:], 'seq', axis=0, tiled=True)  27.3 us
    all_gather x1, waiting for transfers between devices, on_device(): embed_full = lax.all_gather(embed_weight, 'seq', axis=1, tiled=True)  27.2 us
    all_gather x1, blocking collectives, on_device(): lax.all_gather(keyvalue[:, :DK], 'seq', axis=0, tiled=True)  26.4 us
    all_gather x1, blocking collectives, on_device(): lax.all_gather(row_block[:, features:], 'seq', axis=0, tiled=True)  26.4 us
    all_gather x1, waiting for transfers between devices, on_device(): widened = lax.all_gather(padded, 'col', axis=1, tiled=True)  10.3 us
    convert_element_type x2, local copies, waits for them, and re-layouts, on_device(): widened.astype(jnp.float32)  9.6 us
    dot_general x5, matrix products, on_device(): jnp.dot(activated[tap_index:tap_index + positions], conv_weight[tap_index...  8.47 us
  transfers between devices with their start and end apart: 8, of which 4 were waited for; matrix products, arithmetic and copies ran while one was open for 12% of the time, Pallas kernels for 0%

profile of v1, /device:TPU:0, one launch (start us, length us, event | category | flops | bytes accessed | tf_op | source)
XLA Modules:
  0.0 277.9 jit_solution(1666252651280441231)
XLA Ops:
  7.2 1.4 copy.19
  8.7 4.9 %collective-permute-start = (bf16[2,704]{1,0:T(2,128)(2,1)S(1)}, bf16[2,704]{1,0:T(2,128)(2,1)S(1)}, u32[]{:S(2)}, u32[]{:S(2)}) collective-permute-start(bf16[2,704]{1,0:T(2,128)(2,1)S(1)} %get-tuple-element.4), channel_id=1, source_target_pairs={{0,2},{2,4},{4,6},{6,8},{8,10},{10,12},{12,14},{1,3},{3,5},{5,7},{... | collective-permute-start | bytes 8456 | tf_op jit(solution)/shard_map/ppermute | solution.py:24
  14.9 4.2 %collective-permute-done.1 = bf16[2,704]{1,0:T(2,128)(2,1)S(1)} collective-permute-done((bf16[2,704]{1,0:T(2,128)(2,1)S(1)}, bf16[2,704]{1,0:T(2,128)(2,1)S(1)}, u32[]{:S(2)}, u32[]{:S(2)}) %collective-permute-start.1) | collective-permute-done | bytes 2848 | tf_op jit(solution)/shard_map/ppermute | solution.py:25
  21.0 10.3 %all-gather.10.cloned.1.call-done = bf16[2,704,516]{1,2,0:T(8,128)(2,1)} async-done(((bf16[1,704,516]{1,2,0:T(8,128)(2,1)}), bf16[2,704,516]{1,2,0:T(8,128)(2,1)}) %all-gather.10.cloned.1.call-update) | async-done | bytes 1453072 | tf_op jit(solution)/shard_map/all_gather | solution.py:83
  31.4 4.3 %copy.22 = f32[2,704,516]{1,0,2:T(2,128)} copy(bf16[2,704,516]{1,2,0:T(8,128)(2,1)} %all-gather.10.cloned.1.call-done) | data formatting | bytes 4359168 | tf_op jit(solution)/shard_map/convert_element_type | solution.py:85
  35.6 5.3 %reshape.68 = f32[1408,516]{0,1:T(8,128)} reshape(f32[2,704,516]{1,0,2:T(2,128)} %copy.22) | data formatting | bytes 5812224 | tf_op jit(solution)/shard_map/convert_element_type | solution.py:85
  41.0 2.4 multiply_reduce_fusion
  45.1 3.0 %fusion.16 = f32[512,704]{0,1:T(8,128)S(1)} fusion(bf16[5,1408,704]{1,2,0:T(8,128)(2,1)} %param.11, bf16[516,1408]{1,0:T(8,128)(2,1)S(1)} %fusion.7), kind=kOutput, calls=%fused_computation.21 | convolution fusion | flops 1015021568 | bytes 4866048 | tf_op jit(solution)/shard_map/dot_general | solution.py:89
  48.2 1.4 copy-done.5
  53.6 1.5 add_add_fusion
  55.1 1.6 copy.23
  56.7 1.8 reshape.55
  59.4 27.2 %all-gather.6.cloned.1.call-done = bf16[704,1536]{0,1:T(8,128)(2,1)} async-done(((bf16[704,192]{0,1:T(8,128)(2,1)}), bf16[704,1536]{0,1:T(8,128)(2,1)}) %all-gather.6.cloned.1.call-update) | async-done | bytes 2162704 | tf_op jit(solution)/shard_map/all_gather | solution.py:95
  86.6 3.3 %convolution_convert_fusion.1 = bf16[128,1536]{1,0:T(8,128)(2,1)} fusion(bf16[704,1536]{0,1:T(8,128)(2,1)} %all-gather.6.cloned.1.call-done, f32[128,704]{1,0:T(8,128)S(1)} %reduce_sum.46), kind=kOutput, calls=%fused_computation.11 | convolution fusion | flops 277200896 | bytes 2916352 | tf_op jit(solution)/shard_map/dot_general | solution.py:98
  91.2 3.7 %all-to-all-start = ((bf16[8,192,512]{2,1,0:T(8,128)(2,1)}), bf16[8,192,512]{2,1,0:T(8,128)(2,1)S(1)}, u32[]{:S(2)}, u32[]{:S(2)}) async-start(bf16[8,192,512]{2,1,0:T(8,128)(2,1)} %stack.2), calls=%async_computation.1 | async-start | bytes 3145728 | tf_op jit(solution)/shard_map/all_to_all | solution.py:14
  95.9 73.4 %all_gather.30 = bf16[1536,320]{1,0:T(8,128)(2,1)S(1)} all-gather(bf16[192,320]{1,0:T(8,128)(2,1)} %param.16), channel_id=1, replica_groups=mesh['grp'=2,'seq'=8,'col'=2] {'seq'}, dimensions={0}, use_global_device_ids=true | all-gather | bytes 1105920 | tf_op jit(solution)/shard_map/all_gather | solution.py:118
  171.4 2.3 all_gather.29
  175.9 26.4 %all_gather.31 = bf16[1024,128]{0,1:T(8,128)(2,1)S(1)} all-gather(bf16[128,128]{0,1:T(8,128)(2,1)S(1)} %slice.71), channel_id=1, replica_groups=mesh['grp'=2,'seq'=8,'col'=2] {'seq'}, dimensions={0}, use_global_device_ids=true | all-gather | bytes 294912 | tf_op jit(solution)/shard_map/all_gather | solution.py:127
  202.4 27.3 %all_gather.32 = bf16[1024,192]{0,1:T(8,128)(2,1)S(1)} all-gather(bf16[128,192]{0,1:T(8,128)(2,1)S(1)} %slice.72), channel_id=1, replica_groups=mesh['grp'=2,'seq'=8,'col'=2] {'seq'}, dimensions={0}, use_global_device_ids=true | all-gather | bytes 442368 | tf_op jit(solution)/shard_map/all_gather | solution.py:128
  231.8 3.3 %convolution_convert_fusion = bf16[128,1536]{1,0:T(8,128)(2,1)} fusion(bf16[128,768]{1,0:T(8,128)(2,1)S(1)} %reshape.58, bf16[768,1536]{0,1:T(8,128)(2,1)} %all-gather.8.cloned.1.call-done), kind=kOutput, calls=%fused_computation.10 | convolution fusion | flops 302186496 | bytes 2949120 | tf_op jit(solution)/shard_map/dot_general | solution.py:136
  235.1 5.2 %reduce-scatter.5.cloned.1.call-done = bf16[64,1536]{1,0:T(8,128)(2,1)} async-done(((bf16[128,1536]{1,0:T(8,128)(2,1)}), bf16[64,1536]{1,0:T(8,128)(2,1)}) %reduce-scatter.5.cloned.1.call-update) | async-done | bytes 196624 | tf_op jit(solution)/shard_map/reduce_scatter | solution.py:141
  240.4 1.7 convert_reduce_fusion
  242.3 1.8 all-gather.1
  244.1 26.4 %all_gather.35 = bf16[64,128]{1,0:T(8,128)(2,1)S(1)} all-gather(bf16[8,128]{1,0:T(8,128)(2,1)S(1)} %get-tuple-element.7), channel_id=1, replica_groups=mesh['grp'=2,'seq'=8,'col'=2] {'seq'}, dimensions={0}, use_global_device_ids=true | all-gather | bytes 18432 | tf_op jit(solution)/shard_map/all_gather | solution.py:153
  (68 shorter events, 19.6 us)
Async XLA Ops:
  7.2 234.9 %copy-start = (bf16[1536,256]{1,0:T(8,128)(2,1)S(1)}, bf16[1536,256]{1,0:T(8,128)(2,1)}, u32[]{:S(2)}) copy-start(bf16[1536,256]{1,0:T(8,128)(2,1)} %param.18) | copy-start | bytes 2359300
  7.2 24.2 %all-gather.10.cloned.1.call-start = ((), (), s32[]{:S(2)}) async-start(), calls=%async_computation.7 | async-start | bytes 2396160 | tf_op jit(solution)/shard_map/all_gather | solution.py:83
  8.7 6.2 %collective-permute-start = (bf16[2,704]{1,0:T(2,128)(2,1)S(1)}, bf16[2,704]{1,0:T(2,128)(2,1)S(1)}, u32[]{:S(2)}, u32[]{:S(2)}) collective-permute-start(bf16[2,704]{1,0:T(2,128)(2,1)S(1)} %get-tuple-element.4), channel_id=1, source_target_pairs={{0,2},{2,4},{4,6},{6,8},{8,10},{10,12},{12,14},{1,3},{3,5},{5,7},{... | collective-permute-start | bytes 8456 | tf_op jit(solution)/shard_map/ppermute | solution.py:24
  13.6 5.5 %collective-permute-start.1 = (bf16[2,704]{1,0:T(2,128)(2,1)S(1)}, bf16[2,704]{1,0:T(2,128)(2,1)S(1)}, u32[]{:S(2)}, u32[]{:S(2)}) collective-permute-start(bf16[2,704]{1,0:T(2,128)(2,1)S(1)} %get-tuple-element.5), channel_id=1, source_target_pairs={{2,0},{4,2},{6,4},{8,6},{10,8},{12,10},{14,12},{3,1},{5,3},{7,5},{... | collective-permute-start | bytes 8456 | tf_op jit(solution)/shard_map/ppermute | solution.py:25
  20.2 66.3 %all-gather.6.cloned.1.call-start = ((), (), s32[]{:S(2)}) async-start(), calls=%async_computation.3 | async-start | bytes 2654208 | tf_op jit(solution)/shard_map/all_gather | solution.py:95
  21.0 148.3 %reduce-scatter.3.cloned.1.call-start = ((), (), s32[]{:S(2)}) async-start(), calls=%async_computation.4 | async-start | bytes 589824 | tf_op jit(solution)/shard_map/reduce_scatter | solution.py:97
  41.0 2.9 %copy-start.1 = (f32[1408,516]{0,1:T(8,128)S(1)}, f32[1408,516]{0,1:T(8,128)}, u32[]{:S(2)}) copy-start(f32[1408,516]{0,1:T(8,128)} %reshape.68) | copy-start | bytes 8718340
  41.0 2.9 %copy-start.9 = (f32[1408]{0:T(1024)S(1)}, f32[1408]{0:T(1024)}, u32[]{:S(2)}) copy-start(f32[1408]{0:T(1024)} %param.12) | copy-start | bytes 16900
  45.1 4.4 %copy-start.5 = (bf16[5,1408,704]{1,2,0:T(8,128)(2,1)S(1)}, bf16[5,1408,704]{1,2,0:T(8,128)(2,1)}, u32[]{:S(2)}) copy-start(bf16[5,1408,704]{1,2,0:T(8,128)(2,1)} %param.11) | copy-start | bytes 29736964
  52.2 1.4 copy-start.3
  59.4 30.5 %copy-start.7 = (bf16[192,1024]{1,0:T(8,128)(2,1)S(1)}, bf16[192,1024]{1,0:T(8,128)(2,1)}, u32[]{:S(2)}) copy-start(bf16[192,1024]{1,0:T(8,128)(2,1)} %param.15) | copy-start | bytes 1179652
  91.2 3.8 %copy-start.6 = (bf16[1536,192]{0,1:T(8,128)(2,1)S(1)}, bf16[1536,192]{0,1:T(8,128)(2,1)}, u32[]{:S(2)}) copy-start(bf16[1536,192]{0,1:T(8,128)(2,1)} %param.17) | copy-start | bytes 1769476
  91.2 83.2 %all-to-all-start = ((bf16[8,192,512]{2,1,0:T(8,128)(2,1)}), bf16[8,192,512]{2,1,0:T(8,128)(2,1)S(1)}, u32[]{:S(2)}, u32[]{:S(2)}) async-start(bf16[8,192,512]{2,1,0:T(8,128)(2,1)} %stack.2), calls=%async_computation.1 | async-start | bytes 3145728 | tf_op jit(solution)/shard_map/all_to_all | solution.py:14
  94.9 75.4 %copy-start.10 = (f32[1536]{0:T(1024)S(1)}, f32[1536]{0:T(1024)}, u32[]{:S(2)}) copy-start(f32[1536]{0:T(1024)} %param.14) | copy-start | bytes 18436
  95.0 136.8 %all-gather.8.cloned.1.call-start = ((), (), s32[]{:S(2)}) async-start(), calls=%async_computation.5 | async-start | bytes 2654208 | tf_op jit(solution)/shard_map/all_gather | solution.py:138
  95.8 144.6 %reduce-scatter.5.cloned.1.call-start = ((), (), s32[]{:S(2)}) async-start(), calls=%async_computation.6 | async-start | bytes 589824 | tf_op jit(solution)/shard_map/reduce_scatter | solution.py:141
  173.7 0.7 copy-start.2
  231.5 8.9 %copy-start.4 = (bf16[64,1536]{1,0:T(8,128)(2,1)S(1)}, bf16[64,1536]{1,0:T(8,128)(2,1)}, u32[]{:S(2)}) copy-start(bf16[64,1536]{1,0:T(8,128)(2,1)} %reduce-scatter.3.cloned.1.call-done) | copy-start | bytes 589828
  231.8 38.8 %copy-start.8 = (bf16[128,128]{1,0:T(8,128)(2,1)S(1)}, bf16[128,128]{1,0:T(8,128)(2,1)}, u32[]{:S(2)}) copy-start(bf16[128,128]{1,0:T(8,128)(2,1)} %param.19) | copy-start | bytes 98308
Sparse Core Ops, SparseCore 0:
  20.4 10.9 all-gather.9
  33.5 52.9 all-gather.5
  90.0 6.3 reduce-scatter.2
  98.4 83.7 all-gather.7
  235.2 5.0 reduce-scatter.4
